TPU v7x, 32 devices: a whole 2x2x4 slice. The times are simulated.
32 devices in a mesh: gx: 4 (over y, x), gy: 2 (over core), gz: 4 (over z).
Axes of the slice: x: 2, y: 2, z: 4, core: 2. Of those that a mesh axis runs over, the one named last changes fastest.
Arguments:
- state: float32 [5, 16, 32, 512], P(None, 'gx', 'gy', 'gz'), may hold values from -2 to 8, as said below
- volume: float32 [16, 32, 512], P('gx', 'gy', 'gz'), may hold values from 0 to 1, as said below
- apertures: float32 [3, 16, 32, 512], P(None, 'gx', 'gy', 'gz'), may hold values from 0 to 1, as said below
- flags: int32 [16, 32, 512], P('gx', 'gy', 'gz'), may hold values from 0 to 2, as said below
Outputs:
- step_rate: float32 [5, 16, 32, 512], P(None, 'gx', 'gy', 'gz')
Inputs may be any that keep to these rules, and one draw needn't show every extreme that they name: `flags`: in every column of cells the lowest cells are solid (flag 2), one cut cell (flag 1) follows, fluid cells (flag 0) lie above; the cut cell lies between layers 8 and 23. `volume`: 0 in solid cells, between 0.05 and 0.95 in cut cells, 1 in fluid cells; equal to the height of fluid in the cell over a terrain surface. `apertures`: the open part of each face below which the terrain surface lies; lower z faces of solid and cut cells are closed. `state`: density between 0.5 and 2, velocity components between -1 and 1, pressure between 0.5 and 2.
All inputs are finite; a program needn't handle non-finite values.
Results may differ from a plain program's by a relative error of at most 0.0003.
Values sent between devices are 32-bit elements; how exact they have to be, the bound alone decides.
A program may use at most 64 MiB of HBM per device.

v0:
```python
import jax
import jax.numpy as jnp
from jax import lax
from jax.sharding import PartitionSpec as P

CUTZ = 32


GAMMA_LESS = 0.4
DISSIPATION = 4.0
TIME_STEP = 0.02
VOLUME_FLOOR = 0.5


def from_behind(value, axis, steps):
    count = lax.axis_size(axis)
    pairs = [(source, (source + steps) % count) for source in range(count)]
    return lax.ppermute(value, axis, pairs)


def passed_along(array, axis, by):
    size = lax.axis_size(axis)
    pairs = [(i, i + by) for i in range(size) if 0 <= i + by < size]
    return lax.ppermute(array, axis, pairs)


def extended_2(array, sides, width):
    for axis, dim in sides:
        size, length = (lax.axis_size(axis), array.shape[dim])
        up = [(i, (i + 1) % size) for i in range(size)]
        down = [(j, i) for i, j in up]
        last = lax.slice_in_dim(array, length - width, length, axis=dim)
        first = lax.slice_in_dim(array, 0, width, axis=dim)
        before = lax.ppermute(last, axis, up)
        after = lax.ppermute(first, axis, down)
        array = jnp.concatenate([before, array, after], axis=dim)
    return array


def minmod(lower, upper):
    return 0.5 * (jnp.sign(lower) + jnp.sign(upper)) * jnp.minimum(jnp.abs(lower), jnp.abs(upper))


def pressure(cell_state):
    kinetic = (
        cell_state[1] * cell_state[1]
        + cell_state[2] * cell_state[2]
        + cell_state[3] * cell_state[3]
    )
    return GAMMA_LESS * (cell_state[4] - 0.5 * kinetic / cell_state[0])


def physical_flux(cell_state, direction):
    velocity = cell_state[direction] / cell_state[0]
    pressures = pressure(cell_state)
    components = [
        cell_state[direction],
        cell_state[1] * velocity,
        cell_state[2] * velocity,
        cell_state[3] * velocity,
        (cell_state[4] + pressures) * velocity,
    ]
    components[direction] = components[direction] + pressures
    return jnp.stack(components)


def trim_axis(array, dimension, offset, extent):
    return lax.slice_in_dim(array, offset, offset + extent, axis=dimension)


def face_flux(column_part, direction, margin, extent):
    length = column_part.shape[direction]
    differences = trim_axis(column_part, direction, 1, length - 1) - trim_axis(
        column_part, direction, 0, length - 1
    )
    slopes = minmod(
        trim_axis(differences, direction, 0, length - 2),
        trim_axis(differences, direction, 1, length - 2),
    )
    left_state = trim_axis(column_part, direction, margin - 1, extent + 1) + 0.5 * trim_axis(
        slopes, direction, margin - 2, extent + 1
    )
    right_state = trim_axis(column_part, direction, margin, extent + 1) - 0.5 * trim_axis(
        slopes, direction, margin - 1, extent + 1
    )
    average = 0.5 * (physical_flux(left_state, direction) + physical_flux(right_state, direction))
    return average - 0.5 * DISSIPATION * (right_state - left_state)


def section_rate(padded, margin, openings, open_margin, volume, fluid_mask):
    extents = [padded.shape[dimension] - 2 * margin for dimension in (1, 2, 3)]
    centre = padded
    for dimension in (1, 2, 3):
        centre = trim_axis(centre, dimension, margin, extents[dimension - 1])
    pressures = pressure(centre)
    divergence = jnp.zeros_like(centre)
    pushes = []
    for direction in (1, 2, 3):
        column_part = padded
        face_open = openings
        for other_axis in (1, 2, 3):
            if other_axis != direction:
                column_part = trim_axis(column_part, other_axis, margin, extents[other_axis - 1])
                face_open = trim_axis(face_open, other_axis, open_margin, extents[other_axis - 1])
        extent = extents[direction - 1]
        face_open = trim_axis(face_open[direction - 1], direction - 1, open_margin, extent + 1)
        fluxes = face_flux(column_part, direction, margin, extent) * face_open[None]
        divergence = (
            divergence
            + trim_axis(fluxes, direction, 1, extent)
            - trim_axis(fluxes, direction, 0, extent)
        )
        pushes.append(
            pressures
            * (
                trim_axis(face_open, direction - 1, 1, extent)
                - trim_axis(face_open, direction - 1, 0, extent)
            )
        )
    wall_force = jnp.stack([jnp.zeros_like(pressures)] + pushes + [jnp.zeros_like(pressures)])
    return (wall_force - divergence) / jnp.maximum(volume, VOLUME_FLOOR) * fluid_mask


def redistribute(rates, volume, excess):
    moved_sum = jnp.sum(excess[None] * rates, axis=3)
    weight = jnp.sum(volume, axis=2)
    return (1.0 - excess[None]) * rates + volume[None] * (moved_sum / weight[None])[..., None]


def upper_openings(apertures):
    first_x = trim_axis(apertures, 1, 0, 1)
    above_x = from_behind(first_x, "gx", -1)
    extended = jnp.concatenate([jnp.zeros_like(first_x), apertures, above_x], axis=1)
    first_y = trim_axis(extended, 2, 0, 1)
    above_y = from_behind(first_y, "gy", -1)
    extended = jnp.concatenate([jnp.zeros_like(first_y), extended, above_y], axis=2)
    first_z = trim_axis(extended, 3, 0, 1)
    above_z = passed_along(first_z, "gz", -1)
    return jnp.concatenate([jnp.zeros_like(first_z), extended, above_z], axis=3)


def base_rows(rates, volume, excess, offset, at_base):
    slab_rows = trim_axis(rates, 3, offset, CUTZ)
    vol_rows = trim_axis(volume, 2, offset, CUTZ)
    excess_rows = trim_axis(excess, 2, offset, CUTZ)
    redone = lax.cond(
        at_base, lambda: redistribute(slab_rows, vol_rows, excess_rows), lambda: slab_rows
    )
    below = trim_axis(rates, 3, 0, offset)
    above = rates[..., offset + CUTZ :]
    return jnp.concatenate([below, redone, above], axis=3)


def on_device(state, volume, apertures, flags):
    fluid_mask = (flags != 2).astype(jnp.float32)
    excess = (1.0 - volume) * (flags == 1).astype(jnp.float32)
    at_base = lax.axis_index("gz") == 0
    openings = upper_openings(apertures)

    def interior_rate(current):
        padded = extended_2(current, (("gx", 1), ("gy", 2), ("gz", 3)), 2)
        rates = section_rate(padded, 2, openings, 1, volume, fluid_mask)
        return base_rows(rates, volume, excess, 0, at_base)

    first_rate = interior_rate(state)
    second = interior_rate(state + TIME_STEP * first_rate)
    return 0.5 * (first_rate + second)


def solution(mesh):
    in_specs = (
        P(None, "gx", "gy", "gz"),
        P("gx", "gy", "gz"),
        P(None, "gx", "gy", "gz"),
        P("gx", "gy", "gz"),
    )
    out_specs = P(None, "gx", "gy", "gz")
    return jax.shard_map(
        on_device, mesh=mesh, in_specs=in_specs, out_specs=out_specs, check_vma=False
    )
```

profile of v0, /device:TPU:0, one launch (start us, length us, event | category | flops | bytes accessed | tf_op | source)
XLA Modules:
  0.0 88.3 jit_solution(17630679006155631222)
XLA Ops:
  0.0 1.0 %fusion.33 = (f32[5,2,16,128]{3,2,1,0:T(8,128)S(1)}, f32[5,2,16,128]{3,2,1,0:T(8,128)S(1)}) fusion(f32[5,4,16,128]{3,2,1,0:T(8,128)} %param.8), kind=kLoop, calls=%fused_computation.252 | loop fusion | bytes 327680 | tf_op jit(solution)/shard_map/slice | solution.py:33
  1.0 3.0 %collective-permute-start.3 = (f32[5,2,16,128]{3,2,1,0:T(8,128)S(1)}, f32[5,2,16,128]{3,2,1,0:T(8,128)S(1)}, u32[]{:S(2)}, u32[]{:S(2)}) collective-permute-start(f32[5,2,16,128]{3,2,1,0:T(8,128)S(1)} %get-tuple-element.102), channel_id=1, source_target_pairs={{0,8},{8,16},{16,24},{24,0},{1,9},{9,17},{17,25},{25,1},{2,10},{10... | collective-permute-start | bytes 245768 | tf_op jit(solution)/shard_map/ppermute | solution.py:34
  4.0 1.0 %collective-permute-start.4 = (f32[5,2,16,128]{3,2,1,0:T(8,128)S(1)}, f32[5,2,16,128]{3,2,1,0:T(8,128)S(1)}, u32[]{:S(2)}, u32[]{:S(2)}) collective-permute-start(f32[5,2,16,128]{3,2,1,0:T(8,128)S(1)} %get-tuple-element.101), channel_id=1, source_target_pairs={{8,0},{16,8},{24,16},{0,24},{9,1},{17,9},{25,17},{1,25},{10,2},{18... | collective-permute-start | bytes 245768 | tf_op jit(solution)/shard_map/ppermute | solution.py:35
  5.0 2.0 %collective-permute-start = (f32[3,1,16,128]{3,2,1,0:T(8,128)S(1)}, f32[3,1,16,128]{3,2,1,0:T(8,128)S(1)}, u32[]{:S(2)}, u32[]{:S(2)}) collective-permute-start(f32[3,1,16,128]{3,2,1,0:T(8,128)S(1)} %slice.764), channel_id=1, source_target_pairs={{0,24},{8,0},{16,8},{24,16},{1,25},{9,1},{17,9},{25,17},{2,26},{10... | collective-permute-start | bytes 73736 | tf_op jit(solution)/shard_map/ppermute | solution.py:18
  7.0 0.7 copy-done.3
  7.8 0.8 copy-done.2
  8.6 1.4 %collective-permute-done = f32[3,1,16,128]{3,2,1,0:T(8,128)S(1)} collective-permute-done((f32[3,1,16,128]{3,2,1,0:T(8,128)S(1)}, f32[3,1,16,128]{3,2,1,0:T(8,128)S(1)}, u32[]{:S(2)}, u32[]{:S(2)}) %collective-permute-start) | collective-permute-done | bytes 24608 | tf_op jit(solution)/shard_map/ppermute | solution.py:18
  10.1 1.1 %collective-permute-done.1 = f32[3,6,1,128]{3,2,1,0:T(1,128)S(1)} collective-permute-done((f32[3,6,1,128]{3,2,1,0:T(1,128)S(1)}, f32[3,6,1,128]{3,2,1,0:T(1,128)S(1)}, u32[]{:S(2)}, u32[]{:S(2)}) %collective-permute-start.1) | collective-permute-done | bytes 9248 | tf_op jit(solution)/shard_map/ppermute | solution.py:18
  11.2 1.3 %collective-permute-start.2 = (f32[3,6,18,1]{3,2,1,0:T(8,128)S(1)}, f32[3,6,18,1]{3,2,1,0:T(8,128)S(1)}, u32[]{:S(2)}, u32[]{:S(2)}) collective-permute-start(f32[3,6,18,1]{3,2,1,0:T(8,128)S(1)} %pad_maximum_fusion.37), channel_id=1, source_target_pairs={{1,0},{2,1},{3,2},{5,4},{6,5},{7,6},{9,8},{10,9},{11,10},{13,12},{... | collective-permute-start | bytes 3896 | tf_op jit(solution)/shard_map/ppermute | solution.py:24
  12.6 8.0 %collective-permute-done.2 = f32[3,6,18,1]{3,2,1,0:T(8,128)S(1)} collective-permute-done((f32[3,6,18,1]{3,2,1,0:T(8,128)S(1)}, f32[3,6,18,1]{3,2,1,0:T(8,128)S(1)}, u32[]{:S(2)}, u32[]{:S(2)}) %collective-permute-start.2) | collective-permute-done | bytes 1328 | tf_op jit(solution)/shard_map/ppermute | solution.py:24
  21.5 0.5 collective-permute-start.6
  22.0 0.6 collective-permute-done.5
  23.6 1.6 %collective-permute-start.7 = (f32[5,8,20,2]{3,2,1,0:T(8,128)S(1)}, f32[5,8,20,2]{3,2,1,0:T(8,128)S(1)}, u32[]{:S(2)}, u32[]{:S(2)}) collective-permute-start(f32[5,8,20,2]{3,2,1,0:T(8,128)S(1)} %get-tuple-element.89), channel_id=1, source_target_pairs={{0,1},{1,2},{2,3},{3,0},{4,5},{5,6},{6,7},{7,4},{8,9},{9,10},{10,1... | collective-permute-start | bytes 19208 | tf_op jit(solution)/shard_map/ppermute | solution.py:34
  25.2 2.2 %collective-permute-start.8 = (f32[5,8,20,2]{3,2,1,0:T(8,128)S(1)}, f32[5,8,20,2]{3,2,1,0:T(8,128)S(1)}, u32[]{:S(2)}, u32[]{:S(2)}) collective-permute-start(f32[5,8,20,2]{3,2,1,0:T(8,128)S(1)} %get-tuple-element.90), channel_id=1, source_target_pairs={{1,0},{2,1},{3,2},{0,3},{5,4},{6,5},{7,6},{4,7},{9,8},{10,9},{11,1... | collective-permute-start | bytes 19208 | tf_op jit(solution)/shard_map/ppermute | solution.py:35
  27.6 12.0 %collective-permute-done.7 = f32[5,8,20,2]{3,2,1,0:T(8,128)S(1)} collective-permute-done((f32[5,8,20,2]{3,2,1,0:T(8,128)S(1)}, f32[5,8,20,2]{3,2,1,0:T(8,128)S(1)}, u32[]{:S(2)}, u32[]{:S(2)}) %collective-permute-start.7) | collective-permute-done | bytes 6432 | tf_op jit(solution)/shard_map/ppermute | solution.py:34
  39.6 9.4 %collective-permute-done.8 = f32[5,8,20,2]{3,2,1,0:T(8,128)S(1)} collective-permute-done((f32[5,8,20,2]{3,2,1,0:T(8,128)S(1)}, f32[5,8,20,2]{3,2,1,0:T(8,128)S(1)}, u32[]{:S(2)}, u32[]{:S(2)}) %collective-permute-start.8) | collective-permute-done | bytes 6432 | tf_op jit(solution)/shard_map/ppermute | solution.py:35
  48.9 0.4 fusion.5
  49.7 0.3 fusion.4
  50.6 0.4 conditional.2
  51.2 1.8 %collective-permute-start.10 = (f32[5,2,16,128]{3,2,1,0:T(8,128)S(1)}, f32[5,2,16,128]{3,2,1,0:T(8,128)S(1)}, u32[]{:S(2)}, u32[]{:S(2)}) collective-permute-start(f32[5,2,16,128]{3,2,1,0:T(8,128)S(1)} %get-tuple-element.100), channel_id=1, source_target_pairs={{8,0},{16,8},{24,16},{0,24},{9,1},{17,9},{25,17},{1,25},{10,2},{18... | collective-permute-start | bytes 245768 | tf_op jit(solution)/shard_map/ppermute | solution.py:35
  53.4 2.3 %collective-permute-done.10 = f32[5,2,16,128]{3,2,1,0:T(8,128)S(1)} collective-permute-done((f32[5,2,16,128]{3,2,1,0:T(8,128)S(1)}, f32[5,2,16,128]{3,2,1,0:T(8,128)S(1)}, u32[]{:S(2)}, u32[]{:S(2)}) %collective-permute-start.10) | collective-permute-done | bytes 81952 | tf_op jit(solution)/shard_map/ppermute | solution.py:35
  55.6 2.7 %collective-permute-done.9 = f32[5,2,16,128]{3,2,1,0:T(8,128)S(1)} collective-permute-done((f32[5,2,16,128]{3,2,1,0:T(8,128)S(1)}, f32[5,2,16,128]{3,2,1,0:T(8,128)S(1)}, u32[]{:S(2)}, u32[]{:S(2)}) %collective-permute-start.9) | collective-permute-done | bytes 81952 | tf_op jit(solution)/shard_map/ppermute | solution.py:34
  58.8 0.5 collective-permute-start.12
  59.4 0.6 collective-permute-done.11
  61.0 0.7 collective-permute-start.13
  61.7 3.1 %collective-permute-start.14 = (f32[5,8,20,2]{3,2,1,0:T(8,128)S(1)}, f32[5,8,20,2]{3,2,1,0:T(8,128)S(1)}, u32[]{:S(2)}, u32[]{:S(2)}) collective-permute-start(f32[5,8,20,2]{3,2,1,0:T(8,128)S(1)} %get-tuple-element.88), channel_id=1, source_target_pairs={{1,0},{2,1},{3,2},{0,3},{5,4},{6,5},{7,6},{4,7},{9,8},{10,9},{11,1... | collective-permute-start | bytes 19208 | tf_op jit(solution)/shard_map/ppermute | solution.py:35
  64.9 12.0 %collective-permute-done.13 = f32[5,8,20,2]{3,2,1,0:T(8,128)S(1)} collective-permute-done((f32[5,8,20,2]{3,2,1,0:T(8,128)S(1)}, f32[5,8,20,2]{3,2,1,0:T(8,128)S(1)}, u32[]{:S(2)}, u32[]{:S(2)}) %collective-permute-start.13) | collective-permute-done | bytes 6432 | tf_op jit(solution)/shard_map/ppermute | solution.py:34
  77.0 8.5 %collective-permute-done.14 = f32[5,8,20,2]{3,2,1,0:T(8,128)S(1)} collective-permute-done((f32[5,8,20,2]{3,2,1,0:T(8,128)S(1)}, f32[5,8,20,2]{3,2,1,0:T(8,128)S(1)}, u32[]{:S(2)}, u32[]{:S(2)}) %collective-permute-start.14) | collective-permute-done | bytes 6432 | tf_op jit(solution)/shard_map/ppermute | solution.py:35
  85.4 0.4 fusion.2
  86.1 0.3 fusion.1
  87.1 0.4 conditional.3
  87.5 0.8 fusion.20
  (143 shorter events, 6.2 us)
Async XLA Ops:
  0.0 5.0 %copy-start.1 = (f32[3,4,16,128]{3,2,1,0:T(8,128)S(1)}, f32[3,4,16,128]{3,2,1,0:T(8,128)}, u32[]{:S(2)}) copy-start(f32[3,4,16,128]{3,2,1,0:T(8,128)} %param.10) | copy-start | bytes 294916
  1.0 19.9 %collective-permute-start.3 = (f32[5,2,16,128]{3,2,1,0:T(8,128)S(1)}, f32[5,2,16,128]{3,2,1,0:T(8,128)S(1)}, u32[]{:S(2)}, u32[]{:S(2)}) collective-permute-start(f32[5,2,16,128]{3,2,1,0:T(8,128)S(1)} %get-tuple-element.102), channel_id=1, source_target_pairs={{0,8},{8,16},{16,24},{24,0},{1,9},{9,17},{17,25},{25,1},{2,10},{10... | collective-permute-start | bytes 245768 | tf_op jit(solution)/shard_map/ppermute | solution.py:34
  4.0 17.0 %collective-permute-start.4 = (f32[5,2,16,128]{3,2,1,0:T(8,128)S(1)}, f32[5,2,16,128]{3,2,1,0:T(8,128)S(1)}, u32[]{:S(2)}, u32[]{:S(2)}) collective-permute-start(f32[5,2,16,128]{3,2,1,0:T(8,128)S(1)} %get-tuple-element.101), channel_id=1, source_target_pairs={{8,0},{16,8},{24,16},{0,24},{9,1},{17,9},{25,17},{1,25},{10,2},{18... | collective-permute-start | bytes 245768 | tf_op jit(solution)/shard_map/ppermute | solution.py:35
  5.0 4.9 %collective-permute-start = (f32[3,1,16,128]{3,2,1,0:T(8,128)S(1)}, f32[3,1,16,128]{3,2,1,0:T(8,128)S(1)}, u32[]{:S(2)}, u32[]{:S(2)}) collective-permute-start(f32[3,1,16,128]{3,2,1,0:T(8,128)S(1)} %slice.764), channel_id=1, source_target_pairs={{0,24},{8,0},{16,8},{24,16},{1,25},{9,1},{17,9},{25,17},{2,26},{10... | collective-permute-start | bytes 73736 | tf_op jit(solution)/shard_map/ppermute | solution.py:18
  7.0 0.8 copy-start.3
  7.8 0.8 copy-start.2
  8.5 1.5 %copy-start = (f32[5,4,16,128]{3,2,1,0:T(8,128)S(1)}, f32[5,4,16,128]{3,2,1,0:T(8,128)}, u32[]{:S(2)}) copy-start(f32[5,4,16,128]{3,2,1,0:T(8,128)} %param.8) | copy-start | bytes 491524
  9.9 1.2 %collective-permute-start.1 = (f32[3,6,1,128]{3,2,1,0:T(1,128)S(1)}, f32[3,6,1,128]{3,2,1,0:T(1,128)S(1)}, u32[]{:S(2)}, u32[]{:S(2)}) collective-permute-start(f32[3,6,1,128]{3,2,1,0:T(1,128)S(1)} %pad_maximum_fusion.53), channel_id=1, source_target_pairs={{0,4},{4,0},{1,5},{5,1},{2,6},{6,2},{3,7},{7,3},{8,12},{12,8},{9,1... | collective-permute-start | bytes 27656 | tf_op jit(solution)/shard_map/ppermute | solution.py:18
  11.2 9.4 %collective-permute-start.2 = (f32[3,6,18,1]{3,2,1,0:T(8,128)S(1)}, f32[3,6,18,1]{3,2,1,0:T(8,128)S(1)}, u32[]{:S(2)}, u32[]{:S(2)}) collective-permute-start(f32[3,6,18,1]{3,2,1,0:T(8,128)S(1)} %pad_maximum_fusion.37), channel_id=1, source_target_pairs={{1,0},{2,1},{3,2},{5,4},{6,5},{7,6},{9,8},{10,9},{11,10},{13,12},{... | collective-permute-start | bytes 3896 | tf_op jit(solution)/shard_map/ppermute | solution.py:24
  21.4 1.3 %collective-permute-start.5 = (f32[5,8,2,128]{3,2,1,0:T(2,128)S(1)}, f32[5,8,2,128]{3,2,1,0:T(2,128)S(1)}, u32[]{:S(2)}, u32[]{:S(2)}) collective-permute-start(f32[5,8,2,128]{3,2,1,0:T(2,128)S(1)} %get-tuple-element.97), channel_id=1, source_target_pairs={{0,4},{4,0},{1,5},{5,1},{2,6},{6,2},{3,7},{7,3},{8,12},{12,8},{9,1... | collective-permute-start | bytes 122888 | tf_op jit(solution)/shard_map/ppermute | solution.py:34
  21.5 1.4 %collective-permute-start.6 = (f32[5,8,2,128]{3,2,1,0:T(2,128)S(1)}, f32[5,8,2,128]{3,2,1,0:T(2,128)S(1)}, u32[]{:S(2)}, u32[]{:S(2)}) collective-permute-start(f32[5,8,2,128]{3,2,1,0:T(2,128)S(1)} %get-tuple-element.98), channel_id=1, source_target_pairs={{4,0},{0,4},{5,1},{1,5},{6,2},{2,6},{7,3},{3,7},{12,8},{8,12},{13,... | collective-permute-start | bytes 122888 | tf_op jit(solution)/shard_map/ppermute | solution.py:35
  23.6 16.0 %collective-permute-start.7 = (f32[5,8,20,2]{3,2,1,0:T(8,128)S(1)}, f32[5,8,20,2]{3,2,1,0:T(8,128)S(1)}, u32[]{:S(2)}, u32[]{:S(2)}) collective-permute-start(f32[5,8,20,2]{3,2,1,0:T(8,128)S(1)} %get-tuple-element.89), channel_id=1, source_target_pairs={{0,1},{1,2},{2,3},{3,0},{4,5},{5,6},{6,7},{7,4},{8,9},{9,10},{10,1... | collective-permute-start | bytes 19208 | tf_op jit(solution)/shard_map/ppermute | solution.py:34
  25.2 23.7 %collective-permute-start.8 = (f32[5,8,20,2]{3,2,1,0:T(8,128)S(1)}, f32[5,8,20,2]{3,2,1,0:T(8,128)S(1)}, u32[]{:S(2)}, u32[]{:S(2)}) collective-permute-start(f32[5,8,20,2]{3,2,1,0:T(8,128)S(1)} %get-tuple-element.90), channel_id=1, source_target_pairs={{1,0},{2,1},{3,2},{0,3},{5,4},{6,5},{7,6},{4,7},{9,8},{10,9},{11,1... | collective-permute-start | bytes 19208 | tf_op jit(solution)/shard_map/ppermute | solution.py:35
  51.2 4.5 %collective-permute-start.10 = (f32[5,2,16,128]{3,2,1,0:T(8,128)S(1)}, f32[5,2,16,128]{3,2,1,0:T(8,128)S(1)}, u32[]{:S(2)}, u32[]{:S(2)}) collective-permute-start(f32[5,2,16,128]{3,2,1,0:T(8,128)S(1)} %get-tuple-element.100), channel_id=1, source_target_pairs={{8,0},{16,8},{24,16},{0,24},{9,1},{17,9},{25,17},{1,25},{10,2},{18... | collective-permute-start | bytes 245768 | tf_op jit(solution)/shard_map/ppermute | solution.py:35
  53.0 5.3 %collective-permute-start.9 = (f32[5,2,16,128]{3,2,1,0:T(8,128)S(1)}, f32[5,2,16,128]{3,2,1,0:T(8,128)S(1)}, u32[]{:S(2)}, u32[]{:S(2)}) collective-permute-start(f32[5,2,16,128]{3,2,1,0:T(8,128)S(1)} %get-tuple-element.99), channel_id=1, source_target_pairs={{0,8},{8,16},{16,24},{24,0},{1,9},{9,17},{17,25},{25,1},{2,10},{10... | collective-permute-start | bytes 245768 | tf_op jit(solution)/shard_map/ppermute | solution.py:34
  58.7 1.3 %collective-permute-start.11 = (f32[5,8,2,128]{3,2,1,0:T(2,128)S(1)}, f32[5,8,2,128]{3,2,1,0:T(2,128)S(1)}, u32[]{:S(2)}, u32[]{:S(2)}) collective-permute-start(f32[5,8,2,128]{3,2,1,0:T(2,128)S(1)} %get-tuple-element.95), channel_id=1, source_target_pairs={{0,4},{4,0},{1,5},{5,1},{2,6},{6,2},{3,7},{7,3},{8,12},{12,8},{9,1... | collective-permute-start | bytes 122888 | tf_op jit(solution)/shard_map/ppermute | solution.py:34
  58.8 1.4 %collective-permute-start.12 = (f32[5,8,2,128]{3,2,1,0:T(2,128)S(1)}, f32[5,8,2,128]{3,2,1,0:T(2,128)S(1)}, u32[]{:S(2)}, u32[]{:S(2)}) collective-permute-start(f32[5,8,2,128]{3,2,1,0:T(2,128)S(1)} %get-tuple-element.96), channel_id=1, source_target_pairs={{4,0},{0,4},{5,1},{1,5},{6,2},{2,6},{7,3},{3,7},{12,8},{8,12},{13,... | collective-permute-start | bytes 122888 | tf_op jit(solution)/shard_map/ppermute | solution.py:35
  61.0 16.0 %collective-permute-start.13 = (f32[5,8,20,2]{3,2,1,0:T(8,128)S(1)}, f32[5,8,20,2]{3,2,1,0:T(8,128)S(1)}, u32[]{:S(2)}, u32[]{:S(2)}) collective-permute-start(f32[5,8,20,2]{3,2,1,0:T(8,128)S(1)} %get-tuple-element.87), channel_id=1, source_target_pairs={{0,1},{1,2},{2,3},{3,0},{4,5},{5,6},{6,7},{7,4},{8,9},{9,10},{10,1... | collective-permute-start | bytes 19208 | tf_op jit(solution)/shard_map/ppermute | solution.py:34
  61.7 23.7 %collective-permute-start.14 = (f32[5,8,20,2]{3,2,1,0:T(8,128)S(1)}, f32[5,8,20,2]{3,2,1,0:T(8,128)S(1)}, u32[]{:S(2)}, u32[]{:S(2)}) collective-permute-start(f32[5,8,20,2]{3,2,1,0:T(8,128)S(1)} %get-tuple-element.88), channel_id=1, source_target_pairs={{1,0},{2,1},{3,2},{0,3},{5,4},{6,5},{7,6},{4,7},{9,8},{10,9},{11,1... | collective-permute-start | bytes 19208 | tf_op jit(solution)/shard_map/ppermute | solution.py:35
where the time goes:
time: 88.6 us; the launch traced here: 88.3 us
  waiting for transfers between devices  58.9 us (66%)
  starting transfers between devices  18.3 us (21%)
  other arithmetic  6.86 us (8%)
  local copies, waits for them, and re-layouts  3.33 us (4%)
    ppermute x6, waiting for transfers between devices, extended_2(): before = lax.ppermute(last, axis, up)  27.9 us
    ppermute x6, waiting for transfers between devices, extended_2(): after = lax.ppermute(first, axis, down)  20.4 us
    ppermute x6, starting transfers between devices, extended_2(): after = lax.ppermute(first, axis, down)  9.24 us
    ppermute x1, waiting for transfers between devices, passed_along(): return lax.ppermute(array, axis, pairs)  8.04 us
    ppermute x6, starting transfers between devices, extended_2(): before = lax.ppermute(last, axis, up)  5.76 us
    ppermute x2, waiting for transfers between devices, from_behind(): return lax.ppermute(value, axis, pairs)  2.46 us
    ppermute x2, starting transfers between devices, from_behind(): return lax.ppermute(value, axis, pairs)  2.03 us
  transfers between devices with their start and end apart: 15, of which 13 were waited for; matrix products, arithmetic and copies ran while one was open for 1% of the time, Pallas kernels for 0%

commit v1 on v0

v1 whole, which is shorter than its diff:
```python
import jax
import jax.numpy as jnp
from jax import lax
from jax.experimental import pallas as pl
from jax.experimental.pallas import tpu as pltpu
from jax.sharding import PartitionSpec as P

CUTZ = 32
NF = 5
GAMMA_LESS = 0.4
DISSIPATION = 4.0
TIME_STEP = 0.02
VOLUME_FLOOR = 0.5
PAD = 8

MESH = pl.DeviceIdType.MESH


def minmod(a, b):
    return jnp.maximum(jnp.minimum(a, b), 0.0) + jnp.minimum(jnp.maximum(a, b), 0.0)


def pressure_of(w, inverse):
    kinetic = w[1] * w[1] + w[2] * w[2] + w[3] * w[3]
    return GAMMA_LESS * (w[4] - 0.5 * kinetic * inverse)


def flux(w, d):
    inverse = 1.0 / w[0]
    u = w[d] * inverse
    p = pressure_of(w, inverse)
    out = [w[d], w[1] * u, w[2] * u, w[3] * u, (w[4] + p) * u]
    out[d] = out[d] + p
    return out


def face(left, right, d, half_open):
    fl, fr = flux(left, d), flux(right, d)
    return [
        ((fl[f] + fr[f]) + DISSIPATION * (left[f] - right[f])) * half_open for f in range(NF)
    ]


def kernel(
    state, volume, apertures, flags, out,
    buf1, buf2, ox, oy, oz, vol, flg, pk, rec_low, rec_high, gfix, sfix, afix, acc,
    first, scale, keep, gain, local_sem, send_sem, recv_sem,
):
    _, X, Y, Z = state.shape
    F4 = 4 * X
    me = [lax.axis_index(a) for a in ("gx", "gy", "gz")]
    size = [lax.axis_size(a) for a in ("gx", "gy", "gz")]
    up = [{a: lax.rem(me[i] + 1, size[i])} for i, a in enumerate(("gx", "gy", "gz"))]
    down = [{a: lax.rem(me[i] + size[i] - 1, size[i])} for i, a in enumerate(("gx", "gy", "gz"))]

    rows = pl.ds(PAD, Y)
    loads = [
        (state, buf1.at[:, pl.ds(2, X), rows, :]),
        (apertures.at[0], ox.at[pl.ds(0, X)]),
        (apertures.at[1], oy.at[:, pl.ds(0, Y), :]),
        (apertures.at[2], oz),
        (volume, vol),
        (flags, flg),
    ]
    loads = [pltpu.make_async_copy(s, d, local_sem.at[i]) for i, (s, d) in enumerate(loads)]
    for load in loads:
        load.start()

    barrier = pltpu.get_barrier_semaphore()
    for i in range(3):
        pl.semaphore_signal(barrier, inc=1, device_id=up[i], device_id_type=MESH)
        pl.semaphore_signal(barrier, inc=1, device_id=down[i], device_id_type=MESH)
    pl.semaphore_wait(barrier, 6)

    def remote(src, dst, slot, target):
        return pltpu.make_async_remote_copy(
            src_ref=src, dst_ref=dst, send_sem=send_sem.at[slot], recv_sem=recv_sem.at[slot],
            device_id=target, device_id_type=MESH,
        )

    def x_copies(src, x0, r, buf, slot):
        own = lambda lo: src.at[:, pl.ds(x0 + lo, 2), r, :]
        return (
            remote(own(0), buf.at[:, pl.ds(X + 2, 2), rows, :], slot, down[0]),
            remote(own(X - 2), buf.at[:, pl.ds(0, 2), rows, :], slot + 1, up[0]),
        )

    def y_copies(src, x0, y0, buf, slot):
        mid = pl.ds(x0, X)
        return (
            remote(src.at[:, mid, pl.ds(y0, 2), :],
                   buf.at[:, pl.ds(2, X), pl.ds(PAD + Y, 2), :], slot, down[1]),
            remote(src.at[:, mid, pl.ds(y0 + Y - 2, 2), :],
                   buf.at[:, pl.ds(2, X), pl.ds(PAD - 2, 2), :], slot + 1, up[1]),
        )

    def z_copies(stage, slot):
        return (
            remote(pk.at[stage], rec_high.at[stage], slot, down[2]),
            remote(pk.at[stage], rec_low.at[stage], slot + 1, up[2]),
        )

    xs1 = x_copies(state, 0, pl.ds(0, Y), buf1, 0)
    ys1 = y_copies(state, 0, 0, buf1, 2)
    ax = remote(apertures.at[0, pl.ds(0, 1)], ox.at[pl.ds(X, 1)], 4, down[0])
    ay = remote(apertures.at[1, :, pl.ds(0, 1), :], oy.at[:, pl.ds(Y, 1), :], 5, down[1])
    for c in xs1 + ys1 + (ax, ay):
        c.start()
    for load in loads:
        load.wait()

    lane = lax.broadcasted_iota(jnp.int32, (Y, Z), 1)
    quad = lax.rem(lane, 4)

    def pack(buf, stage):
        packed = jnp.zeros((Y, Z), jnp.float32)
        for f in range(NF + 1):
            for x in range(X):
                base = f * F4 + 4 * x
                value = buf[f, x + 2, PAD:PAD + Y, :] if f < NF else oz[x]
                inside = (lane >= base) & (lane < base + 4)
                packed = jnp.where(inside, pltpu.roll(value, base + 2, 1), packed)
        pk[stage] = packed

    pack(buf1, 0)
    zs1 = z_copies(0, 6)
    for c in zs1:
        c.start()

    limit = jnp.where(me[2] == 0, CUTZ, 0)
    for x in range(X):
        v = vol[x]
        fl = flg[x]
        weight = jnp.sum(jnp.where(lane < CUTZ, v, 0.0), axis=1, keepdims=True)
        excess = jnp.where((fl == 1) & (lane < limit), 1.0 - v, 0.0)
        scale[x] = jnp.where(fl != 2, 1.0 / jnp.maximum(v, VOLUME_FLOOR), 0.0)
        keep[x] = excess
        gain[x] = jnp.where(lane < limit, v / weight, 0.0)

    def boundary_z(stage):
        own, low, high = pk[stage], rec_low[stage], rec_high[stage]
        lefts, rights, slopes = [], [], []
        for c in (jnp.where(quad < 2, own, high), jnp.where(quad < 2, low, own)):
            d = c - pltpu.roll(c, 1, 1)
            s = minmod(d, pltpu.roll(d, Z - 1, 1))
            slopes.append(s)
            lefts.append(c + 0.5 * s)
            rights.append(c - 0.5 * s)
        top = quad == 0
        left = jnp.where(top, pltpu.roll(lefts[0], Z - 1, 1), lefts[1])
        right = jnp.where(
            top, pltpu.roll(rights[0], Z - 2, 1), pltpu.roll(rights[1], Z - 1, 1)
        )
        sfix[...] = jnp.where(
            top, pltpu.roll(slopes[0], Z - 1, 1), pltpu.roll(slopes[1], Z - 1, 1)
        )
        opening = jnp.where(
            top, pltpu.roll(high, Z - 2, 1), pltpu.roll(own, Z - 1, 1)
        )
        ls = [pltpu.roll(left, Z - f * F4, 1) if f else left for f in range(NF)]
        rs = [pltpu.roll(right, Z - f * F4, 1) if f else right for f in range(NF)]
        opening = pltpu.roll(opening, Z - NF * F4, 1)
        live = lane < F4
        ls = [jnp.where(live & (quad < 2), w, 1.0) for w in ls]
        rs = [jnp.where(live & (quad < 2), w, 1.0) for w in rs]
        g = face(ls, rs, 3, 0.5 * opening)
        for f in range(NF):
            gfix[f] = g[f]
        afix[...] = opening

    def yz_part(x, buf):
        v = [buf[f, x + 2, PAD:PAD + Y, :] for f in range(NF)]
        p = pressure_of(v, 1.0 / v[0])
        a = oz[x]
        shift = Z - (4 * x + 1)
        sl = []
        for f in range(NF):
            d = v[f] - pltpu.roll(v[f], 1, 1)
            s = minmod(d, pltpu.roll(d, Z - 1, 1))
            fix = pltpu.roll(sfix[...], lax.rem(2 * Z - (f * F4 + 4 * x + 1), Z), 1)
            sl.append(0.5 * jnp.where((lane == 0) | (lane == Z - 1), fix, s))
        left = [pltpu.roll(v[f] + sl[f], 1, 1) for f in range(NF)]
        right = [v[f] - sl[f] for f in range(NF)]
        g = face(left, right, 3, 0.5 * a)
        div = []
        for f in range(NF):
            fix = pltpu.roll(gfix[f], shift, 1)
            low = jnp.where(lane == 0, fix, g[f])
            high = jnp.where(lane == Z - 1, fix, pltpu.roll(g[f], Z - 1, 1))
            div.append(high - low)
        a_high = jnp.where(
            lane == Z - 1, pltpu.roll(afix[...], shift, 1), pltpu.roll(a, Z - 1, 1)
        )
        div[3] = div[3] - p * (a_high - a)
        E = Y + 8
        left, right = [], []
        for f in range(NF):
            c = buf[f, x + 2, PAD - 1:PAD - 1 + E, :]
            b = buf[f, x + 2, PAD - 2:PAD - 2 + E, :]
            n = buf[f, x + 2, PAD:PAD + E, :]
            s = 0.5 * minmod(c - b, n - c)
            left.append(c + s)
            right.append(pltpu.roll(c - s, E - 1, 0))
        a = oy[x]
        g = face(left, right, 2, 0.5 * a)
        for f in range(NF):
            div[f] = div[f] + (pltpu.roll(g[f], E - 1, 0)[:Y] - g[f][:Y])
        div[2] = div[2] - p * (oy[x, 1:Y + 1, :] - oy[x, 0:Y, :])
        div[1] = div[1] - p * (ox[x + 1] - ox[x])
        for f in range(NF):
            acc[f, x] = div[f]

    def x_part(buf, finish):
        def load(f, x):
            return buf[f, x + 2, PAD:PAD + Y, :]

        def half_slope(x):
            return [
                0.5 * minmod(load(f, x) - load(f, x - 1), load(f, x + 1) - load(f, x))
                for f in range(NF)
            ]

        s = half_slope(-1)
        left = [load(f, -1) + s[f] for f in range(NF)]
        below = None
        for x in range(X + 1):
            s = half_slope(x)
            right = [load(f, x) - s[f] for f in range(NF)]
            g = face(left, right, 1, 0.5 * ox[x])
            left = [load(f, x) + s[f] for f in range(NF)]
            if x > 0:
                c = x - 1
                rates = []
                for f in range(NF):
                    base = -(acc[f, c] + (g[f] - below[f])) * scale[c]
                    moved = jnp.sum(keep[c] * base, axis=1, keepdims=True)
                    rates.append((1.0 - keep[c]) * base + gain[c] * moved)
                finish(c, rates)
            below = g

    def yz_loop(buf):
        def body(x, carry):
            yz_part(x, buf)
            return carry

        lax.fori_loop(0, X, body, 0)

    def arrive(copies):
        for c in copies:
            c.wait_recv()

    arrive(zs1 + ys1 + (ax, ay))
    boundary_z(0)
    yz_loop(buf1)
    arrive(xs1)

    xs2 = x_copies(buf2, 2, rows, buf2, 8)
    ys2 = y_copies(buf2, 2, PAD, buf2, 10)
    zs2 = z_copies(1, 12)

    def finish_first(c, rates):
        for f in range(NF):
            first[f, c] = rates[f]
            buf2[f, c + 2, PAD:PAD + Y, :] = buf1[f, c + 2, PAD:PAD + Y, :] + TIME_STEP * rates[f]
        if c == 1:
            xs2[0].start()
        if c == X - 1:
            xs2[1].start()

    x_part(buf1, finish_first)
    for c in ys2:
        c.start()
    pack(buf2, 1)
    for c in zs2:
        c.start()

    arrive(zs2 + ys2)
    boundary_z(1)
    yz_loop(buf2)
    arrive(xs2)

    def finish_second(c, rates):
        for f in range(NF):
            out[f, c] = 0.5 * (first[f, c] + rates[f])

    x_part(buf2, finish_second)
    for c in xs1 + ys1 + zs1 + (ax, ay) + xs2 + ys2 + zs2:
        c.wait_send()


def on_device(state, volume, apertures, flags):
    _, X, Y, Z = state.shape
    f32 = jnp.float32
    wide = pltpu.VMEM((NF, X + 4, Y + 2 * PAD, Z), f32)
    cells = pltpu.VMEM((X, Y, Z), f32)
    fields = pltpu.VMEM((NF, X, Y, Z), f32)
    layer = pltpu.VMEM((Y, Z), f32)
    pair = pltpu.VMEM((2, Y, Z), f32)
    return pl.pallas_call(
        kernel,
        out_shape=jax.ShapeDtypeStruct(state.shape, f32),
        in_specs=[pl.BlockSpec(memory_space=pl.ANY)] * 4,
        out_specs=pl.BlockSpec(memory_space=pltpu.VMEM),
        scratch_shapes=[
            wide, wide,
            pltpu.VMEM((X + 1, Y, Z), f32),
            pltpu.VMEM((X, Y + 8, Z), f32),
            cells, cells, pltpu.VMEM((X, Y, Z), jnp.int32),
            pair, pair, pair,
            pltpu.VMEM((NF, Y, Z), f32), layer, layer,
            fields, fields, cells, cells, cells,
            pltpu.SemaphoreType.DMA((6,)),
            pltpu.SemaphoreType.DMA((14,)),
            pltpu.SemaphoreType.DMA((14,)),
        ],
        compiler_params=pltpu.CompilerParams(collective_id=0, has_side_effects=True),
    )(state, volume, apertures, flags)


def solution(mesh):
    in_specs = (
        P(None, "gx", "gy", "gz"),
        P("gx", "gy", "gz"),
        P(None, "gx", "gy", "gz"),
        P("gx", "gy", "gz"),
    )
    return jax.shard_map(
        on_device, mesh=mesh, in_specs=in_specs, out_specs=P(None, "gx", "gy", "gz"),
        check_vma=False,
    )
```

time: 88.6 us -> 20.6 us (0.23)
  waiting for transfers between devices: 58.9 us -> 0 us
  Pallas kernels: 0 us -> 18.8 us
  starting transfers between devices: 18.3 us -> 0 us
  other arithmetic: 6.86 us -> 0 us
  local copies, waits for them, and re-layouts: 3.33 us -> 1.59 us
    ppermute x15 -> x0, waiting for transfers between devices: 58.9 us -> none  [the longest x6 27.9 us: extended_2(): before = lax.ppermute(last, axis, up)]
    pallas_call x0 -> x1, Pallas kernels: none -> 18.8 us  [on_device(): pl.pallas_call(kernel, out_shape=jax.ShapeDtypeStruct(state.shape, f32),...]
    ppermute x15 -> x0, starting transfers between devices: 18.3 us -> none  [the longest x6 9.24 us: extended_2(): after = lax.ppermute(first, axis, down)]
    mul x15 -> x0, other arithmetic: 2.71 us -> none  [the longest x6 1.07 us: minmod(): 0.5 * (jnp.sign(lower) + jnp.sign(upper))]
    slice x10 -> x0, local copies, waits for them, and re-layouts: 1.69 us -> none  [the longest x1 0.97 us: extended_2(): first = lax.slice_in_dim(array, 0, width, axis=dim)]
    add x9 -> x0, other arithmetic: 1.27 us -> none  [the longest x6 0.89 us: face_flux(): trim_axis(column_part, direction, margin - 1, extent + 1)]
    sub x8 -> x0, other arithmetic: 1 us -> none  [the longest x6 0.99 us: face_flux(): trim_axis(column_part, direction, 1, length - 1)]
    unnamed x42 -> x0, other arithmetic: 0.92 us -> none
  transfers between devices with their start and end apart: 15 -> 0, of which waited for: 13 -> 0; matrix products, arithmetic and copies ran while one was open for 1% -> 0% of each run, Pallas kernels for 0% -> 0%
where the time goes in v1:
time: 20.6 us; the launch traced here: 20.4 us
  Pallas kernels  18.8 us (91%)
  local copies, waits for them, and re-layouts  1.59 us (8%)
    pallas_call x1, Pallas kernels, on_device(): pl.pallas_call(kernel, out_shape=jax.ShapeDtypeStruct(state.shape, f32),...  18.8 us
    unnamed x1, local copies, waits for them, and re-layouts  1.59 us

profile of v1, /device:TPU:0, one launch (start us, length us, event | category | flops | bytes accessed | tf_op | source)
XLA Modules:
  0.0 20.4 jit_solution(7387805437862352049)
XLA Ops:
  0.0 18.8 %shard_map.46 = f32[5,4,16,128]{3,2,1,0:T(8,128)} custom-call(f32[5,4,16,128]{3,2,1,0:T(8,128)} %state.1, f32[4,16,128]{2,1,0:T(8,128)} %volume.1, f32[3,4,16,128]{3,2,1,0:T(8,128)} %apertures.1, s32[4,16,128]{2,1,0:T(8,128)} %flags.1), custom_call_target="tpu_custom_call" | custom-call | tf_op jit(solution)/shard_map/pallas_call | solution.py:299
  18.9 1.6 %copy.6 = f32[5,4,16,128]{3,2,1,0:T(8,128)} copy(f32[5,4,16,128]{3,2,1,0:T(8,128)} %shard_map.46) | data formatting | bytes 327680

commit v2 on v1

--- a/solution.py
+++ b/solution.py
@@ -44,7 +44,7 @@
 def kernel(
     state, volume, apertures, flags, out,
     buf1, buf2, ox, oy, oz, vol, flg, pk, rec_low, rec_high, gfix, sfix, afix, acc,
-    first, scale, keep, gain, local_sem, send_sem, recv_sem,
+    first, scale, keep, gain, local_sem, send_sem, recv_sem, chain,
 ):
     _, X, Y, Z = state.shape
     F4 = 4 * X
@@ -67,10 +67,21 @@
         load.start()
 
     barrier = pltpu.get_barrier_semaphore()
-    for i in range(3):
+    n_z = size[2]
+    bottom, top = me[2] == 0, me[2] == n_z - 1
+    for i in range(2):
         pl.semaphore_signal(barrier, inc=1, device_id=up[i], device_id_type=MESH)
         pl.semaphore_signal(barrier, inc=1, device_id=down[i], device_id_type=MESH)
-    pl.semaphore_wait(barrier, 6)
+
+    @pl.when(jnp.logical_not(top))
+    def _():
+        pl.semaphore_signal(barrier, inc=1, device_id=up[2], device_id_type=MESH)
+
+    @pl.when(jnp.logical_not(bottom))
+    def _():
+        pl.semaphore_signal(barrier, inc=1, device_id=down[2], device_id_type=MESH)
+
+    pl.semaphore_wait(barrier, 6 - jnp.where(top, 1, 0) - jnp.where(bottom, 1, 0))
 
     def remote(src, dst, slot, target):
         return pltpu.make_async_remote_copy(
@@ -124,8 +135,27 @@
 
     pack(buf1, 0)
     zs1 = z_copies(0, 6)
-    for c in zs1:
-        c.start()
+
+    @pl.when(jnp.logical_not(bottom))
+    def _():
+        zs1[0].start()
+
+    @pl.when(jnp.logical_not(top))
+    def _():
+        zs1[1].start()
+
+    if n_z > 2:
+        @pl.when(me[2] < n_z - 2)
+        def _():
+            pl.semaphore_wait(chain, 1)
+
+        @pl.when((me[2] > 0) & (me[2] < n_z - 1))
+        def _():
+            pl.semaphore_signal(chain, inc=1, device_id=down[2], device_id_type=MESH)
+
+    @pl.when(bottom)
+    def _():
+        zs1[0].start()
 
     limit = jnp.where(me[2] == 0, CUTZ, 0)
     for x in range(X):
@@ -138,7 +168,10 @@
         gain[x] = jnp.where(lane < limit, v / weight, 0.0)
 
     def boundary_z(stage):
-        own, low, high = pk[stage], rec_low[stage], rec_high[stage]
+        own = pk[stage]
+        still = jnp.where(quad == 0, pltpu.roll(own, Z - 2, 1), pltpu.roll(own, Z - 1, 1))
+        low = jnp.where(bottom, still, rec_low[stage])
+        high = rec_high[0] if stage == 0 else jnp.where(top, rec_high[0], rec_high[stage])
         lefts, rights, slopes = [], [], []
         for c in (jnp.where(quad < 2, own, high), jnp.where(quad < 2, low, own)):
             d = c - pltpu.roll(c, 1, 1)
@@ -146,16 +179,16 @@
             slopes.append(s)
             lefts.append(c + 0.5 * s)
             rights.append(c - 0.5 * s)
-        top = quad == 0
-        left = jnp.where(top, pltpu.roll(lefts[0], Z - 1, 1), lefts[1])
+        first_lane = quad == 0
+        left = jnp.where(first_lane, pltpu.roll(lefts[0], Z - 1, 1), lefts[1])
         right = jnp.where(
-            top, pltpu.roll(rights[0], Z - 2, 1), pltpu.roll(rights[1], Z - 1, 1)
+            first_lane, pltpu.roll(rights[0], Z - 2, 1), pltpu.roll(rights[1], Z - 1, 1)
         )
         sfix[...] = jnp.where(
-            top, pltpu.roll(slopes[0], Z - 1, 1), pltpu.roll(slopes[1], Z - 1, 1)
+            first_lane, pltpu.roll(slopes[0], Z - 1, 1), pltpu.roll(slopes[1], Z - 1, 1)
         )
         opening = jnp.where(
-            top, pltpu.roll(high, Z - 2, 1), pltpu.roll(own, Z - 1, 1)
+            first_lane, pltpu.roll(high, Z - 2, 1), pltpu.roll(own, Z - 1, 1)
         )
         ls = [pltpu.roll(left, Z - f * F4, 1) if f else left for f in range(NF)]
         rs = [pltpu.roll(right, Z - f * F4, 1) if f else right for f in range(NF)]
@@ -168,7 +201,7 @@
             gfix[f] = g[f]
         afix[...] = opening
 
-    def yz_part(x, buf):
+    def z_part(x, buf):
         v = [buf[f, x + 2, PAD:PAD + Y, :] for f in range(NF)]
         p = pressure_of(v, 1.0 / v[0])
         a = oz[x]
@@ -182,18 +215,24 @@
         left = [pltpu.roll(v[f] + sl[f], 1, 1) for f in range(NF)]
         right = [v[f] - sl[f] for f in range(NF)]
         g = face(left, right, 3, 0.5 * a)
-        div = []
+        div = [acc[f, x] for f in range(NF)]
         for f in range(NF):
             fix = pltpu.roll(gfix[f], shift, 1)
             low = jnp.where(lane == 0, fix, g[f])
             high = jnp.where(lane == Z - 1, fix, pltpu.roll(g[f], Z - 1, 1))
-            div.append(high - low)
+            div[f] = div[f] + (high - low)
         a_high = jnp.where(
             lane == Z - 1, pltpu.roll(afix[...], shift, 1), pltpu.roll(a, Z - 1, 1)
         )
         div[3] = div[3] - p * (a_high - a)
+        for f in range(NF):
+            acc[f, x] = div[f]
+
+    def y_part(x, buf):
+        v = [buf[f, x + 2, PAD:PAD + Y, :] for f in range(NF)]
+        p = pressure_of(v, 1.0 / v[0])
         E = Y + 8
-        left, right = [], []
+        left, right, div = [], [], []
         for f in range(NF):
             c = buf[f, x + 2, PAD - 1:PAD - 1 + E, :]
             b = buf[f, x + 2, PAD - 2:PAD - 2 + E, :]
@@ -204,7 +243,7 @@
         a = oy[x]
         g = face(left, right, 2, 0.5 * a)
         for f in range(NF):
-            div[f] = div[f] + (pltpu.roll(g[f], E - 1, 0)[:Y] - g[f][:Y])
+            div.append(pltpu.roll(g[f], E - 1, 0)[:Y] - g[f][:Y])
         div[2] = div[2] - p * (oy[x, 1:Y + 1, :] - oy[x, 0:Y, :])
         div[1] = div[1] - p * (ox[x + 1] - ox[x])
         for f in range(NF):
@@ -238,9 +277,9 @@
                 finish(c, rates)
             below = g
 
-    def yz_loop(buf):
+    def loop(part, buf):
         def body(x, carry):
-            yz_part(x, buf)
+            part(x, buf)
             return carry
 
         lax.fori_loop(0, X, body, 0)
@@ -249,9 +288,16 @@
         for c in copies:
             c.wait_recv()
 
-    arrive(zs1 + ys1 + (ax, ay))
+    arrive(ys1 + (ax, ay))
+    loop(y_part, buf1)
+    zs1[0].wait_recv()
+
+    @pl.when(jnp.logical_not(bottom))
+    def _():
+        zs1[1].wait_recv()
+
     boundary_z(0)
-    yz_loop(buf1)
+    loop(z_part, buf1)
     arrive(xs1)
 
     xs2 = x_copies(buf2, 2, rows, buf2, 8)
@@ -271,12 +317,28 @@
     for c in ys2:
         c.start()
     pack(buf2, 1)
-    for c in zs2:
-        c.start()
-
-    arrive(zs2 + ys2)
+
+    @pl.when(jnp.logical_not(bottom))
+    def _():
+        zs2[0].start()
+
+    @pl.when(jnp.logical_not(top))
+    def _():
+        zs2[1].start()
+
+    arrive(ys2)
+    loop(y_part, buf2)
+
+    @pl.when(jnp.logical_not(top))
+    def _():
+        zs2[0].wait_recv()
+
+    @pl.when(jnp.logical_not(bottom))
+    def _():
+        zs2[1].wait_recv()
+
     boundary_z(1)
-    yz_loop(buf2)
+    loop(z_part, buf2)
     arrive(xs2)
 
     def finish_second(c, rates):
@@ -284,8 +346,17 @@
             out[f, c] = 0.5 * (first[f, c] + rates[f])
 
     x_part(buf2, finish_second)
-    for c in xs1 + ys1 + zs1 + (ax, ay) + xs2 + ys2 + zs2:
+    for c in xs1 + ys1 + (ax, ay, zs1[0]) + xs2 + ys2:
         c.wait_send()
+
+    @pl.when(jnp.logical_not(top))
+    def _():
+        zs1[1].wait_send()
+        zs2[1].wait_send()
+
+    @pl.when(jnp.logical_not(bottom))
+    def _():
+        zs2[0].wait_send()
 
 
 def on_device(state, volume, apertures, flags):
@@ -312,6 +383,7 @@
             pltpu.SemaphoreType.DMA((6,)),
             pltpu.SemaphoreType.DMA((14,)),
             pltpu.SemaphoreType.DMA((14,)),
+            pltpu.SemaphoreType.REGULAR,
         ],
         compiler_params=pltpu.CompilerParams(collective_id=0, has_side_effects=True),
     )(state, volume, apertures, flags)

time: 20.6 us -> 19.5 us (0.947)
  Pallas kernels: 18.8 us -> 17.8 us
    pallas_call x1, Pallas kernels: 18.8 us -> 17.8 us  [on_device(): pl.pallas_call(kernel, out_shape=jax.ShapeDtypeStruct(state.shape, f32),...]
where the time goes in v2:
time: 19.5 us; the launch traced here: 19.4 us
  Pallas kernels  17.8 us (91%)
  local copies, waits for them, and re-layouts  1.59 us (8%)
    pallas_call x1, Pallas kernels, on_device(): pl.pallas_call(kernel, out_shape=jax.ShapeDtypeStruct(state.shape, f32),...  17.8 us
    unnamed x1, local copies, waits for them, and re-layouts  1.59 us

profile of v2, /device:TPU:0, one launch (start us, length us, event | category | flops | bytes accessed | tf_op | source)
XLA Modules:
  0.0 19.4 jit_solution(4792459913832123348)
XLA Ops:
  0.0 17.8 %shard_map.46 = f32[5,4,16,128]{3,2,1,0:T(8,128)} custom-call(f32[5,4,16,128]{3,2,1,0:T(8,128)} %state.1, f32[4,16,128]{2,1,0:T(8,128)} %volume.1, f32[3,4,16,128]{3,2,1,0:T(8,128)} %apertures.1, s32[4,16,128]{2,1,0:T(8,128)} %flags.1), custom_call_target="tpu_custom_call" | custom-call | tf_op jit(solution)/shard_map/pallas_call | solution.py:370
  17.8 1.6 %copy.6 = f32[5,4,16,128]{3,2,1,0:T(8,128)} copy(f32[5,4,16,128]{3,2,1,0:T(8,128)} %shard_map.46) | data formatting | bytes 327680

commit v3 on v2

--- a/solution.py
+++ b/solution.py
@@ -44,7 +44,7 @@
 def kernel(
     state, volume, apertures, flags, out,
     buf1, buf2, ox, oy, oz, vol, flg, pk, rec_low, rec_high, gfix, sfix, afix, acc,
-    first, scale, keep, gain, local_sem, send_sem, recv_sem, chain,
+    first, scale, keep, gain, local_sem, send_sem, recv_sem, chain, press,
 ):
     _, X, Y, Z = state.shape
     F4 = 4 * X
@@ -115,7 +115,7 @@
     ys1 = y_copies(state, 0, 0, buf1, 2)
     ax = remote(apertures.at[0, pl.ds(0, 1)], ox.at[pl.ds(X, 1)], 4, down[0])
     ay = remote(apertures.at[1, :, pl.ds(0, 1), :], oy.at[:, pl.ds(Y, 1), :], 5, down[1])
-    for c in xs1 + ys1 + (ax, ay):
+    for c in (ax,) + xs1 + (ay,) + ys1:
         c.start()
     for load in loads:
         load.wait()
@@ -203,7 +203,7 @@
 
     def z_part(x, buf):
         v = [buf[f, x + 2, PAD:PAD + Y, :] for f in range(NF)]
-        p = pressure_of(v, 1.0 / v[0])
+        p = press[x]
         a = oz[x]
         shift = Z - (4 * x + 1)
         sl = []
@@ -245,7 +245,7 @@
         for f in range(NF):
             div.append(pltpu.roll(g[f], E - 1, 0)[:Y] - g[f][:Y])
         div[2] = div[2] - p * (oy[x, 1:Y + 1, :] - oy[x, 0:Y, :])
-        div[1] = div[1] - p * (ox[x + 1] - ox[x])
+        press[x] = p
         for f in range(NF):
             acc[f, x] = div[f]
 
@@ -271,7 +271,10 @@
                 c = x - 1
                 rates = []
                 for f in range(NF):
-                    base = -(acc[f, c] + (g[f] - below[f])) * scale[c]
+                    total = acc[f, c] + (g[f] - below[f])
+                    if f == 1:
+                        total = total - press[c] * (ox[x] - ox[c])
+                    base = -total * scale[c]
                     moved = jnp.sum(keep[c] * base, axis=1, keepdims=True)
                     rates.append((1.0 - keep[c]) * base + gain[c] * moved)
                 finish(c, rates)
@@ -288,7 +291,7 @@
         for c in copies:
             c.wait_recv()
 
-    arrive(ys1 + (ax, ay))
+    arrive(ys1 + (ay,))
     loop(y_part, buf1)
     zs1[0].wait_recv()
 
@@ -298,7 +301,7 @@
 
     boundary_z(0)
     loop(z_part, buf1)
-    arrive(xs1)
+    arrive((ax,) + xs1)
 
     xs2 = x_copies(buf2, 2, rows, buf2, 8)
     ys2 = y_copies(buf2, 2, PAD, buf2, 10)
@@ -369,7 +372,7 @@
     pair = pltpu.VMEM((2, Y, Z), f32)
     return pl.pallas_call(
         kernel,
-        out_shape=jax.ShapeDtypeStruct(state.shape, f32),
+        out_shape=pltpu.VMEM(state.shape, f32),
         in_specs=[pl.BlockSpec(memory_space=pl.ANY)] * 4,
         out_specs=pl.BlockSpec(memory_space=pltpu.VMEM),
         scratch_shapes=[
@@ -384,6 +387,7 @@
             pltpu.SemaphoreType.DMA((14,)),
             pltpu.SemaphoreType.DMA((14,)),
             pltpu.SemaphoreType.REGULAR,
+            cells,
         ],
         compiler_params=pltpu.CompilerParams(collective_id=0, has_side_effects=True),
     )(state, volume, apertures, flags)

time: 19.5 us -> 16.5 us (0.85)
  Pallas kernels: 17.8 us -> 15.7 us
  local copies, waits for them, and re-layouts: 1.59 us -> 0.67 us
    pallas_call x1, Pallas kernels: 17.8 us -> 15.7 us  [on_device(): pl.pallas_call(kernel, out_shape=pltpu.VMEM(state.shape, f32), in_specs=[...]
    unnamed x1, local copies, waits for them, and re-layouts: 1.59 us -> 0.67 us
where the time goes in v3:
time: 16.5 us; the launch traced here: 16.4 us
  Pallas kernels  15.7 us (95%)
  local copies, waits for them, and re-layouts  0.67 us (4%)
    pallas_call x1, Pallas kernels, on_device(): pl.pallas_call(kernel, out_shape=pltpu.VMEM(state.shape, f32), in_specs=[...  15.7 us
    unnamed x1, local copies, waits for them, and re-layouts  0.67 us

profile of v3, /device:TPU:0, one launch (start us, length us, event | category | flops | bytes accessed | tf_op | source)
XLA Modules:
  0.0 16.4 jit_solution(13515623854484966678)
XLA Ops:
  0.0 15.7 %shard_map.46 = f32[5,4,16,128]{3,2,1,0:T(8,128)S(1)} custom-call(f32[5,4,16,128]{3,2,1,0:T(8,128)} %state.1, f32[4,16,128]{2,1,0:T(8,128)} %volume.1, f32[3,4,16,128]{3,2,1,0:T(8,128)} %apertures.1, s32[4,16,128]{2,1,0:T(8,128)} %flags.1), custom_call_target="tpu_custom_call" | custom-call | tf_op jit(solution)/shard_map/pallas_call | solution.py:373
  15.7 0.7 %copy.6 = f32[5,4,16,128]{3,2,1,0:T(8,128)} copy(f32[5,4,16,128]{3,2,1,0:T(8,128)S(1)} %shard_map.46) | data formatting | bytes 327680

commit v4 on v3

--- a/solution.py
+++ b/solution.py
@@ -285,7 +285,7 @@
             part(x, buf)
             return carry
 
-        lax.fori_loop(0, X, body, 0)
+        lax.fori_loop(0, X, body, 0, unroll=True)
 
     def arrive(copies):
         for c in copies:

time: 16.5 us -> 15.6 us (0.945)
  Pallas kernels: 15.7 us -> 14.7 us
    pallas_call x1, Pallas kernels: 15.7 us -> 14.7 us  [on_device(): pl.pallas_call(kernel, out_shape=pltpu.VMEM(state.shape, f32), in_specs=[...]
where the time goes in v4:
time: 15.6 us; the launch traced here: 15.4 us
  Pallas kernels  14.7 us (94%)
  local copies, waits for them, and re-layouts  0.67 us (4%)
    pallas_call x1, Pallas kernels, on_device(): pl.pallas_call(kernel, out_shape=pltpu.VMEM(state.shape, f32), in_specs=[...  14.7 us
    unnamed x1, local copies, waits for them, and re-layouts  0.67 us

profile of v4, /device:TPU:0, one launch (start us, length us, event | category | flops | bytes accessed | tf_op | source)
XLA Modules:
  0.0 15.4 jit_solution(7604550845126640128)
XLA Ops:
  0.0 14.7 %shard_map.46 = f32[5,4,16,128]{3,2,1,0:T(8,128)S(1)} custom-call(f32[5,4,16,128]{3,2,1,0:T(8,128)} %state.1, f32[4,16,128]{2,1,0:T(8,128)} %volume.1, f32[3,4,16,128]{3,2,1,0:T(8,128)} %apertures.1, s32[4,16,128]{2,1,0:T(8,128)} %flags.1), custom_call_target="tpu_custom_call" | custom-call | tf_op jit(solution)/shard_map/pallas_call | solution.py:373
  14.7 0.7 %copy.6 = f32[5,4,16,128]{3,2,1,0:T(8,128)} copy(f32[5,4,16,128]{3,2,1,0:T(8,128)S(1)} %shard_map.46) | data formatting | bytes 327680

commit v5 on v4

--- a/solution.py
+++ b/solution.py
@@ -44,7 +44,7 @@
 def kernel(
     state, volume, apertures, flags, out,
     buf1, buf2, ox, oy, oz, vol, flg, pk, rec_low, rec_high, gfix, sfix, afix, acc,
-    first, scale, keep, gain, local_sem, send_sem, recv_sem, chain, press,
+    first, scale, keep, gain, local_sem, send_sem, recv_sem, chain, press, inner,
 ):
     _, X, Y, Z = state.shape
     F4 = 4 * X
@@ -201,6 +201,13 @@
             gfix[f] = g[f]
         afix[...] = opening
 
+    def local_part(x, buf):
+        v = [buf[f, x + 2, PAD:PAD + Y, :] for f in range(NF)]
+        press[x] = pressure_of(v, 1.0 / v[0])
+        for f in range(NF):
+            d = v[f] - pltpu.roll(v[f], 1, 1)
+            inner[f, x] = minmod(d, pltpu.roll(d, Z - 1, 1))
+
     def z_part(x, buf):
         v = [buf[f, x + 2, PAD:PAD + Y, :] for f in range(NF)]
         p = press[x]
@@ -208,8 +215,7 @@
         shift = Z - (4 * x + 1)
         sl = []
         for f in range(NF):
-            d = v[f] - pltpu.roll(v[f], 1, 1)
-            s = minmod(d, pltpu.roll(d, Z - 1, 1))
+            s = inner[f, x]
             fix = pltpu.roll(sfix[...], lax.rem(2 * Z - (f * F4 + 4 * x + 1), Z), 1)
             sl.append(0.5 * jnp.where((lane == 0) | (lane == Z - 1), fix, s))
         left = [pltpu.roll(v[f] + sl[f], 1, 1) for f in range(NF)]
@@ -229,8 +235,7 @@
             acc[f, x] = div[f]
 
     def y_part(x, buf):
-        v = [buf[f, x + 2, PAD:PAD + Y, :] for f in range(NF)]
-        p = pressure_of(v, 1.0 / v[0])
+        p = press[x]
         E = Y + 8
         left, right, div = [], [], []
         for f in range(NF):
@@ -245,7 +250,6 @@
         for f in range(NF):
             div.append(pltpu.roll(g[f], E - 1, 0)[:Y] - g[f][:Y])
         div[2] = div[2] - p * (oy[x, 1:Y + 1, :] - oy[x, 0:Y, :])
-        press[x] = p
         for f in range(NF):
             acc[f, x] = div[f]
 
@@ -291,6 +295,7 @@
         for c in copies:
             c.wait_recv()
 
+    loop(local_part, buf1)
     arrive(ys1 + (ay,))
     loop(y_part, buf1)
     zs1[0].wait_recv()
@@ -329,6 +334,7 @@
     def _():
         zs2[1].start()
 
+    loop(local_part, buf2)
     arrive(ys2)
     loop(y_part, buf2)
 
@@ -387,7 +393,7 @@
             pltpu.SemaphoreType.DMA((14,)),
             pltpu.SemaphoreType.DMA((14,)),
             pltpu.SemaphoreType.REGULAR,
-            cells,
+            cells, fields,
         ],
         compiler_params=pltpu.CompilerParams(collective_id=0, has_side_effects=True),
     )(state, volume, apertures, flags)

time: 15.6 us -> 15.5 us (level)
  no operation moved by 1% of the time
where the time goes in v5:
time: 15.5 us; the launch traced here: 15.4 us
  Pallas kernels  14.7 us (95%)
  local copies, waits for them, and re-layouts  0.67 us (4%)
    pallas_call x1, Pallas kernels, on_device(): pl.pallas_call(kernel, out_shape=pltpu.VMEM(state.shape, f32), in_specs=[...  14.7 us
    unnamed x1, local copies, waits for them, and re-layouts  0.67 us

profile of v5, /device:TPU:0, one launch (start us, length us, event | category | flops | bytes accessed | tf_op | source)
XLA Modules:
  0.0 15.4 jit_solution(15795944993335563092)
XLA Ops:
  0.0 14.7 %shard_map.46 = f32[5,4,16,128]{3,2,1,0:T(8,128)S(1)} custom-call(f32[5,4,16,128]{3,2,1,0:T(8,128)} %state.1, f32[4,16,128]{2,1,0:T(8,128)} %volume.1, f32[3,4,16,128]{3,2,1,0:T(8,128)} %apertures.1, s32[4,16,128]{2,1,0:T(8,128)} %flags.1), custom_call_target="tpu_custom_call" | custom-call | tf_op jit(solution)/shard_map/pallas_call | solution.py:379
  14.7 0.7 %copy.6 = f32[5,4,16,128]{3,2,1,0:T(8,128)} copy(f32[5,4,16,128]{3,2,1,0:T(8,128)S(1)} %shard_map.46) | data formatting | bytes 327680
